TPU v7x, 128 devices: a whole 4x4x4 slice. The times are simulated.
128 devices in a mesh: section: 2 (over core), dp: 4 (over x), mp: 16 (over z, y).
Axes of the slice: x: 4, y: 4, z: 4, core: 2. Of those that a mesh axis runs over, the one named last changes fastest.
Arguments:
- segment_input: bfloat16 [2, 4, 256, 2048], P(None, 'dp', None, 'mp'), may hold values from -6 to 6
- out_grad: bfloat16 [2, 4, 256, 2048], P(None, 'dp', None, 'mp'), may hold values from -6 to 6
- pool_tokens: bfloat16 [16, 4, 128, 896], P('section', 'dp'), may hold values from -6 to 6
- neighbour_ids: int32 [2, 4, 4, 4], P(None, 'dp'), may hold values from 0 to 15, as said below
- neighbour_counts: int32 [2, 4, 4], P(None, 'dp'), may hold values from 1 to 4
- enc_gain: float32 [896], replicated, may hold values from 0.5 to 1.5
- enc_up: bfloat16 [896, 4096], P(None, 'mp'), may hold values from -0.1875 to 0.1875
- enc_down: bfloat16 [4096, 896], P(None, 'mp'), may hold values from -0.09375 to 0.09375
- norm_gain: float32 [2, 2048], P('section'), may hold values from 0.5 to 1.5
- w_query: bfloat16 [2, 2048, 4096], P('section', None, 'mp'), may hold values from -0.125 to 0.125
- w_key: bfloat16 [2, 896, 4096], P('section', None, 'mp'), may hold values from -0.1875 to 0.1875
- w_value: bfloat16 [2, 896, 4096], P('section', None, 'mp'), may hold values from -0.1875 to 0.1875
- w_out: bfloat16 [2, 4096, 2048], P('section', None, 'mp'), may hold values from -0.09375 to 0.09375
Outputs:
- grad_key: bfloat16 [2, 896, 4096], P('section', None, 'mp')
- grad_value: bfloat16 [2, 896, 4096], P('section', None, 'mp')
Inputs may be any that keep to these rules, and one draw needn't show every extreme that they name: `neighbour_ids`: the 4 slots of one stretch name distinct pool stretches.
All inputs are finite; a program needn't handle non-finite values.
Results may differ from a plain program's by a relative error of at most 0.025.
Values may be sent and summed in bfloat16 or wider, within the bound.
A program may use at most 128 MiB of HBM per device.

v0:
```python
import jax
import jax.numpy as jnp
from jax import lax
from jax.sharding import PartitionSpec as P

HEAD = 128
NT = 128
EPSILON = 1e-05


def passed_along(value, axis, by):
    peers = lax.axis_size(axis)
    pairs = [(i, i + by) for i in range(peers) if 0 <= i + by < peers]
    return lax.ppermute(value, axis, pairs)


def rms_scale(values):
    return lax.rsqrt(jnp.mean(values * values, axis=-1, keepdims=True) + EPSILON)


def collect(tensor):
    return lax.all_gather(tensor, "mp", axis=1, tiled=True)


def collect_pair(first, second):
    return (
        lax.all_gather(first, "mp", axis=1, tiled=True),
        lax.all_gather(second, "mp", axis=1, tiled=True),
    )


def pass_on(tensor, offset):
    return passed_along(tensor, "section", offset)


def attend(queries, key_block, value_block, usable):
    scores = jnp.einsum("cqhe,ckhe->chqk", queries, key_block, preferred_element_type=jnp.float32)
    scores = jnp.where(usable[:, None, None, :], scores, -1e30)
    weights = jax.nn.softmax(scores, axis=-1)
    weights_bf = weights.astype(jnp.bfloat16)
    attended = jnp.einsum(
        "chqk,ckhe->cqhe", weights_bf, value_block, preferred_element_type=jnp.float32
    )
    return (weights, weights_bf, attended.astype(jnp.bfloat16))


def attend_back(queries, key_block, value_block, weights, weights_bf, grad_attended):
    grad_weights = jnp.einsum(
        "cqhe,ckhe->chqk", grad_attended, value_block, preferred_element_type=jnp.float32
    )
    grad_scores = weights * (grad_weights - jnp.sum(weights * grad_weights, axis=-1, keepdims=True))
    grad_values = jnp.einsum(
        "chqk,cqhe->ckhe", weights_bf, grad_attended, preferred_element_type=jnp.float32
    ).astype(jnp.bfloat16)
    grad_keys = jnp.einsum("chqk,cqhe->ckhe", grad_scores, queries.astype(jnp.float32)).astype(
        jnp.bfloat16
    )
    grad_queries = jnp.einsum("chqk,ckhe->cqhe", grad_scores, key_block.astype(jnp.float32))
    return (grad_keys, grad_values, grad_queries)


def front(rows_in, gain_full, query_cols, key_block, value_block, usable, head_count):
    rows_wide = rows_in.astype(jnp.float32)
    inv_rms = rms_scale(rows_wide)
    normed = (rows_wide * inv_rms * gain_full).astype(jnp.bfloat16)
    query_raw = jnp.dot(normed, query_cols, preferred_element_type=jnp.float32)
    queries = (query_raw * HEAD ** (-0.5)).astype(jnp.bfloat16)
    queries = queries.reshape(key_block.shape[0], -1, head_count, HEAD)
    weights, weights_bf, attended = attend(queries, key_block, value_block, usable)
    return (inv_rms, query_raw, queries, weights, weights_bf, attended)


def on_device(
    segment_input,
    out_grad,
    pool_tokens,
    neighbour_ids,
    neighbour_counts,
    enc_gain,
    enc_up,
    enc_down,
    norm_gain,
    w_query,
    w_key,
    w_value,
    w_out,
):
    model_count = lax.axis_size("mp")
    model_index = lax.axis_index("mp")
    segment_count = lax.axis_size("section")
    segment_index = lax.axis_index("section")
    micro_count = segment_input.shape[0]
    row_count = segment_input.shape[2]
    feat_count = segment_input.shape[3]
    width = feat_count * model_count
    head_count = w_query.shape[2] // HEAD
    tract_count = neighbour_ids.shape[2]
    key_span = neighbour_ids.shape[3] * NT
    raw_rows = pool_tokens[:, 0].reshape(-1, pool_tokens.shape[3])
    raw_wide = raw_rows.astype(jnp.float32)
    enc_normed = (raw_wide * rms_scale(raw_wide) * enc_gain).astype(jnp.bfloat16)
    hidden_part = jax.nn.gelu(
        jnp.dot(enc_normed, enc_up, preferred_element_type=jnp.float32)
    ).astype(jnp.bfloat16)
    hidden_full = collect(hidden_part)
    enc_feat = enc_down.shape[1]
    raw_slice = lax.dynamic_slice_in_dim(raw_wide, model_index * enc_feat, enc_feat, 1)
    encoded = (
        raw_slice + jnp.dot(hidden_full, enc_down, preferred_element_type=jnp.float32)
    ).astype(jnp.bfloat16)
    slot_ids = neighbour_ids[:, 0].reshape(-1)
    shard_rows = encoded.shape[0]
    token_index = jnp.arange(NT, dtype=jnp.int32)
    global_rows = ((slot_ids * NT)[:, None] + token_index[None, :]).reshape(-1)
    empty_pool = jnp.zeros((segment_count * shard_rows, enc_feat * model_count), jnp.bfloat16)
    portion = lax.all_gather(encoded, ("section", "mp"), axis=0, tiled=True)
    shard_total = portion.shape[0] // shard_rows

    def one_shard(position, whole_pool):
        shard_block = lax.dynamic_slice_in_dim(portion, position * shard_rows, shard_rows, 0)
        row_start = position // model_count * shard_rows
        col_start = position % model_count * enc_feat
        return lax.dynamic_update_slice(whole_pool, shard_block, (row_start, col_start))

    whole_pool = lax.fori_loop(0, shard_total, one_shard, empty_pool)
    neighbours = jnp.take(whole_pool, global_rows, axis=0)

    def project(weight):
        projected = jnp.dot(neighbours, weight[0], preferred_element_type=jnp.float32).astype(
            jnp.bfloat16
        )
        return projected.reshape(micro_count, tract_count, key_span, head_count, HEAD)

    key_all = project(w_key)
    value_all = project(w_value)
    span_index = jnp.arange(key_span, dtype=jnp.int32) // NT
    usable_all = span_index[None, None, :] < neighbour_counts[:, 0][:, :, None]
    query_cols = w_query[0]
    out_cols = w_out[0]
    query_rows, out_rows = (
        lax.all_to_all(query_cols, "mp", split_axis=0, concat_axis=1, tiled=True),
        lax.all_to_all(out_cols, "mp", split_axis=0, concat_axis=1, tiled=True),
    )
    gain_full = norm_gain[0]
    gain_own = lax.dynamic_slice_in_dim(gain_full, model_index * feat_count, feat_count, 0)
    inputs_own = segment_input[:, 0]
    grads_own = out_grad[:, 0]
    step_count = micro_count + segment_count - 1
    empty_share = jnp.zeros((row_count, feat_count), jnp.bfloat16)
    stored_start = jnp.zeros((micro_count, row_count, width), jnp.bfloat16)

    def forward_step(step, state):
        received, stored = state
        which = step - segment_index
        active = (which >= 0) & (which < micro_count)
        which = jnp.clip(which, 0, micro_count - 1)
        incoming = jnp.where(segment_index == 0, inputs_own[which], received)
        rows_full = collect(incoming)
        outputs = front(
            rows_full,
            gain_full,
            query_cols,
            key_all[which],
            value_all[which],
            usable_all[which],
            head_count,
        )
        attended = collect(outputs[5].reshape(row_count, -1))
        result = incoming.astype(jnp.float32) + jnp.dot(
            attended, out_cols, preferred_element_type=jnp.float32
        )
        stored = stored.at[which].set(jnp.where(active, rows_full, stored[which]))
        return (pass_on(result.astype(jnp.bfloat16), 1), stored)

    _, stored = lax.fori_loop(0, step_count, forward_step, (empty_share, stored_start))
    grad_start = jnp.zeros((micro_count, tract_count, key_span, head_count, HEAD), jnp.bfloat16)

    def backward_step(step, state):
        received, key_grads, value_grads = state
        which = step - (segment_count - 1 - segment_index)
        active = (which >= 0) & (which < micro_count)
        which = jnp.clip(which, 0, micro_count - 1)
        incoming = jnp.where(segment_index == segment_count - 1, grads_own[which], received)
        rows_full = stored[which]
        rows_own = lax.dynamic_slice_in_dim(rows_full, model_index * feat_count, feat_count, 1)
        key_block = key_all[which]
        value_block = value_all[which]
        inv_rms, query_raw, queries, weights, weights_bf, _ = front(
            rows_full, gain_full, query_cols, key_block, value_block, usable_all[which], head_count
        )
        grad_full = collect(incoming)
        grad_att = jnp.dot(grad_full, out_rows.T, preferred_element_type=jnp.float32).astype(
            jnp.bfloat16
        )
        grad_att = grad_att.reshape(queries.shape)
        grad_keys, grad_values, grad_queries = attend_back(
            queries, key_block, value_block, weights, weights_bf, grad_att
        )
        grad_scaled = (grad_queries * HEAD ** (-0.5)).reshape(row_count, -1).astype(jnp.bfloat16)
        part_total = jnp.sum(
            grad_scaled.astype(jnp.float32) * query_raw, axis=1, keepdims=True
        ).astype(jnp.bfloat16)
        scaled_full, totals = collect_pair(grad_scaled, part_total)
        row_total = jnp.sum(totals.astype(jnp.float32), axis=1, keepdims=True)
        grad_normed = jnp.dot(scaled_full, query_rows.T, preferred_element_type=jnp.float32)
        rows_wide = rows_own.astype(jnp.float32)
        grad_in = (
            incoming.astype(jnp.float32)
            + inv_rms * gain_own * grad_normed
            - rows_wide * inv_rms * inv_rms * row_total / width
        )
        key_grads = key_grads.at[which].set(jnp.where(active, grad_keys, key_grads[which]))
        value_grads = value_grads.at[which].set(jnp.where(active, grad_values, value_grads[which]))
        return (pass_on(grad_in.astype(jnp.bfloat16), -1), key_grads, value_grads)

    _, key_grads, value_grads = lax.fori_loop(
        0, step_count, backward_step, (empty_share, grad_start, grad_start)
    )
    contract = (((0,), (0,)), ((), ()))
    key_sum = lax.dot_general(
        neighbours,
        key_grads.reshape(-1, head_count * HEAD),
        contract,
        preferred_element_type=jnp.float32,
    )
    value_sum = lax.dot_general(
        neighbours,
        value_grads.reshape(-1, head_count * HEAD),
        contract,
        preferred_element_type=jnp.float32,
    )
    key_total, value_total = (
        lax.psum(key_sum.astype(jnp.bfloat16), "dp").astype(jnp.float32),
        lax.psum(value_sum.astype(jnp.bfloat16), "dp").astype(jnp.float32),
    )
    return (key_total.astype(jnp.bfloat16)[None], value_total.astype(jnp.bfloat16)[None])


def solution(mesh):
    placed = (
        P(None, "dp", None, "mp"),
        P(None, "dp", None, "mp"),
        P("section", "dp", None, None),
        P(None, "dp", None, None),
        P(None, "dp", None),
        P(),
        P(None, "mp"),
        P(None, "mp"),
        P("section", None),
        P("section", None, "mp"),
        P("section", None, "mp"),
        P("section", None, "mp"),
        P("section", None, "mp"),
    )
    return jax.shard_map(
        on_device,
        mesh=mesh,
        in_specs=placed,
        out_specs=(P("section", None, "mp"), P("section", None, "mp")),
        check_vma=False,
    )
```

profile of v0, /device:TPU:0, one launch (start us, length us, event | category | flops | bytes accessed | tf_op | source)
XLA Modules:
  0.0 1101.6 jit_solution(5113289207940649873)
XLA Ops:
  16.3 80.0 %all-gather.10.cloned.1.call-done = bf16[1024,4096]{1,0:T(8,128)(2,1)} async-done(((bf16[1024,256]{1,0:T(8,128)(2,1)}), bf16[1024,4096]{1,0:T(8,128)(2,1)}) %all-gather.10.cloned.1.call-update) | async-done | bytes 8388624 | tf_op jit(solution)/shard_map/all_gather | solution.py:22
  96.3 6.7 fusion.104
  103.0 5.1 all-to-all-start
  108.5 17.1 %all-to-all-done = bf16[16,256,128]{2,1,0:T(8,128)(2,1)S(1)} async-done(((bf16[16,256,128]{2,1,0:T(8,128)(2,1)}), bf16[16,256,128]{2,1,0:T(8,128)(2,1)S(1)}, u32[]{:S(2)}, u32[]{:S(2)}) %all-to-all-start) | async-done | bytes 1048608 | tf_op jit(solution)/shard_map/all_to_all | solution.py:142
  133.1 13.0 %all-to-all-done.1 = bf16[16,128,256]{2,1,0:T(8,128)(2,1)S(1)} async-done(((bf16[16,128,256]{2,1,0:T(8,128)(2,1)}), bf16[16,128,256]{2,1,0:T(8,128)(2,1)S(1)}, u32[]{:S(2)}, u32[]{:S(2)}) %all-to-all-start.1) | async-done | bytes 1048608 | tf_op jit(solution)/shard_map/all_to_all | solution.py:141
  148.1 6.3 all-gather.12.cloned.1.call-done
  156.6 184.6 %while.54 = (s32[]{:T(128)}, bf16[2048,896]{1,0:T(8,128)(2,1)}, bf16[32768,56]{0,1:T(8,128)(2,1)}, s32[]{:T(128)}, s32[]{:T(128)}, /*index=5*/s32[]{:T(128)}, s3...) while((s32[]{:T(128)}, bf16[2048,896]{1,0:T(8,128)(2,1)}, ...), condition=%wide.region_2.3_spmd, body=%wide.region_1.2_spmd.sunk | while | flops 26 | bytes 688530 | solution.py:125
  157.7 4.6 dynamic_update_slice.11
  163.4 5.2 dynamic_update_slice.11
  169.7 5.2 dynamic_update_slice.11
  176.0 5.2 dynamic_update_slice.11
  182.3 5.2 dynamic_update_slice.11
  188.6 5.3 dynamic_update_slice.11
  195.0 5.3 dynamic_update_slice.11
  201.3 5.2 dynamic_update_slice.11
  207.7 5.2 dynamic_update_slice.11
  214.0 5.2 dynamic_update_slice.11
  220.3 5.2 dynamic_update_slice.11
  226.6 5.2 dynamic_update_slice.11
  232.9 5.2 dynamic_update_slice.11
  239.2 5.2 dynamic_update_slice.11
  245.5 4.6 dynamic_update_slice.11
  251.2 4.6 dynamic_update_slice.11
  261.6 4.3 dynamic_update_slice.11
  267.1 4.3 dynamic_update_slice.11
  272.5 4.3 dynamic_update_slice.11
  277.9 4.3 dynamic_update_slice.11
  283.3 4.3 dynamic_update_slice.11
  341.2 22.4 %gather_fusion = bf16[4096,896]{1,0:T(8,128)(2,1)} fusion(bf16[2048,896]{1,0:T(8,128)(2,1)} %get-tuple-element.835, s32[4096]{0:T(1024)S(1)} %broadcast_clamp_fusion), kind=kCustom, calls=%fused_computation | custom fusion | bytes 14696448 | tf_op jit(solution)/shard_map/jit(_take)/gather | solution.py:126
  363.6 5.8 convolution_convert_fusion.4
  373.8 5.7 convolution_convert_fusion.5
  385.3 318.6 %while.55 = (s32[]{:T(128)}, bf16[256,128]{1,0:T(8,128)(2,1)S(1)}, bf16[2,256,2048]{2,1,0:T(8,128)(2,1)}, pred[]{:T(512)}, s32[]{:T(128)}, /*index=5*/bf16[2,256...) while((s32[]{:T(128)}, bf16[256,128]{1,0:T(8,128)(2,1)S(1)}, ...), condition=%wide.region_8.9_spmd, body=%wide.region_3.8_spmd.sunk | while | flops 677446400 | bytes 32006564 | solution.py:175
  386.1 45.0 %all-gather.14.cloned.1.call-done = bf16[256,2048]{1,0:T(8,128)(2,1)} async-done(((bf16[256,128]{1,0:T(8,128)(2,1)}), bf16[256,2048]{1,0:T(8,128)(2,1)}) %all-gather.14.cloned.1.call-update) | async-done | bytes 1048592 | tf_op jit(solution)/shard_map/while/body/eval_jaxpr/all_gather | solution.py:22
  441.1 44.5 %all-gather.16.cloned.1.call-done = bf16[256,4096]{1,0:T(8,128)(2,1)} async-done(((bf16[256,256]{1,0:T(8,128)(2,1)}), bf16[256,4096]{1,0:T(8,128)(2,1)}) %all-gather.16.cloned.1.call-update) | async-done | bytes 2097168 | tf_op jit(solution)/shard_map/while/body/eval_jaxpr/all_gather | solution.py:22
  492.2 45.0 %all-gather.14.cloned.1.call-done = bf16[256,2048]{1,0:T(8,128)(2,1)} async-done(((bf16[256,128]{1,0:T(8,128)(2,1)}), bf16[256,2048]{1,0:T(8,128)(2,1)}) %all-gather.14.cloned.1.call-update) | async-done | bytes 1048592 | tf_op jit(solution)/shard_map/while/body/eval_jaxpr/all_gather | solution.py:22
  547.2 44.5 %all-gather.16.cloned.1.call-done = bf16[256,4096]{1,0:T(8,128)(2,1)} async-done(((bf16[256,256]{1,0:T(8,128)(2,1)}), bf16[256,4096]{1,0:T(8,128)(2,1)}) %all-gather.16.cloned.1.call-update) | async-done | bytes 2097168 | tf_op jit(solution)/shard_map/while/body/eval_jaxpr/all_gather | solution.py:22
  598.3 45.2 %all-gather.14.cloned.1.call-done = bf16[256,2048]{1,0:T(8,128)(2,1)} async-done(((bf16[256,128]{1,0:T(8,128)(2,1)}), bf16[256,2048]{1,0:T(8,128)(2,1)}) %all-gather.14.cloned.1.call-update) | async-done | bytes 1048592 | tf_op jit(solution)/shard_map/while/body/eval_jaxpr/all_gather | solution.py:22
  653.6 44.5 %all-gather.16.cloned.1.call-done = bf16[256,4096]{1,0:T(8,128)(2,1)} async-done(((bf16[256,256]{1,0:T(8,128)(2,1)}), bf16[256,4096]{1,0:T(8,128)(2,1)}) %all-gather.16.cloned.1.call-update) | async-done | bytes 2097168 | tf_op jit(solution)/shard_map/while/body/eval_jaxpr/all_gather | solution.py:22
  708.8 323.1 %while.56 = (s32[]{:T(128)}, bf16[256,128]{1,0:T(8,128)(2,1)S(1)}, bf16[2,4,512,2,128]{4,3,2,1,0:T(2,128)(2,1)}, bf16[2,4,512,2,128]{4,3,2,1,0:T(2,128)(2,1)}, p...) while((s32[]{:T(128)}, bf16[256,128]{1,0:T(8,128)(2,1)S(1)}, ...), condition=%wide.region_17.18_spmd, body=%wide.region_9.17_spmd.sunk | while | flops 1152261888 | bytes 76540544 | solution.py:216
  715.5 39.3 %all-gather.18.cloned.1.call-done = bf16[256,2048]{1,0:T(8,128)(2,1)} async-done(((bf16[256,128]{1,0:T(8,128)(2,1)}), bf16[256,2048]{1,0:T(8,128)(2,1)}) %all-gather.18.cloned.1.call-update) | async-done | bytes 1048592 | tf_op jit(solution)/shard_map/while/body/eval_jaxpr/all_gather | solution.py:22
  782.7 22.8 %all-gather.2 = bf16[16,1,256]{2,1,0:T(2,128)(2,1)S(1)} all-gather(bf16[1,1,256]{2,1,0:T(2,128)(2,1)S(1)} %reshape.462), channel_id=1, replica_groups=mesh['section'=2,'dp'=4,'mp'=16] {'mp'}, dimensions={0}, use_global_device_ids=true | all-gather | bytes 8704 | tf_op jit(solution)/shard_map/while/body/eval_jaxpr/all_gather | solution.py:28
  822.7 40.1 %all-gather.18.cloned.1.call-done = bf16[256,2048]{1,0:T(8,128)(2,1)} async-done(((bf16[256,128]{1,0:T(8,128)(2,1)}), bf16[256,2048]{1,0:T(8,128)(2,1)}) %all-gather.18.cloned.1.call-update) | async-done | bytes 1048592 | tf_op jit(solution)/shard_map/while/body/eval_jaxpr/all_gather | solution.py:22
  890.7 22.8 %all-gather.2 = bf16[16,1,256]{2,1,0:T(2,128)(2,1)S(1)} all-gather(bf16[1,1,256]{2,1,0:T(2,128)(2,1)S(1)} %reshape.462), channel_id=1, replica_groups=mesh['section'=2,'dp'=4,'mp'=16] {'mp'}, dimensions={0}, use_global_device_ids=true | all-gather | bytes 8704 | tf_op jit(solution)/shard_map/while/body/eval_jaxpr/all_gather | solution.py:28
  930.7 40.1 %all-gather.18.cloned.1.call-done = bf16[256,2048]{1,0:T(8,128)(2,1)} async-done(((bf16[256,128]{1,0:T(8,128)(2,1)}), bf16[256,2048]{1,0:T(8,128)(2,1)}) %all-gather.18.cloned.1.call-update) | async-done | bytes 1048592 | tf_op jit(solution)/shard_map/while/body/eval_jaxpr/all_gather | solution.py:22
  998.7 22.8 %all-gather.2 = bf16[16,1,256]{2,1,0:T(2,128)(2,1)S(1)} all-gather(bf16[1,1,256]{2,1,0:T(2,128)(2,1)S(1)} %reshape.462), channel_id=1, replica_groups=mesh['section'=2,'dp'=4,'mp'=16] {'mp'}, dimensions={0}, use_global_device_ids=true | all-gather | bytes 8704 | tf_op jit(solution)/shard_map/while/body/eval_jaxpr/all_gather | solution.py:28
  1031.9 7.4 fusion.101
  1039.3 6.7 fusion.98
  1046.1 45.3 %all-reduce.3.cloned.1.call-done = (bf16[1,896,256]{2,1,0:T(8,128)(2,1)}, bf16[1,896,256]{2,1,0:T(8,128)(2,1)}) async-done(((bf16[1,896,256]{2,1,0:T(8,128)(2,1)}, bf16[1,896,256]{2,1,0:T(8,128)(2,1)}), (bf16[1,896,256]{2,1,0:T(8,128)(2,1)}, bf16[1,896,256]{2,1,0:T(8,128)(2,1)})) %all-reduce.3.cloned.1.call-update) | async-done | bytes 917520 | tf_op jit(solution)/shard_map/psum | solution.py:233
  (354 shorter events, 304.4 us)
Async XLA Ops:
  7.2 356.4 %copy-start = (bf16[1,896,256]{2,1,0:T(8,128)(2,1)S(1)}, bf16[1,896,256]{2,1,0:T(8,128)(2,1)}, u32[]{:S(2)}) copy-start(bf16[1,896,256]{2,1,0:T(8,128)(2,1)} %param.35) | copy-start | bytes 1376260
  7.2 89.1 %all-gather.10.cloned.1.call-start = ((), (), s32[]{:S(2)}) async-start(), calls=%async_computation.2 | async-start | bytes 8912896 | tf_op jit(solution)/shard_map/all_gather | solution.py:22
  9.3 2.9 copy-start.16
  12.3 84.0 %copy-start.12 = (bf16[4096,56]{0,1:T(8,128)(2,1)S(1)}, bf16[4096,56]{0,1:T(8,128)(2,1)}, u32[]{:S(2)}) copy-start(bf16[4096,56]{0,1:T(8,128)(2,1)} %param.32) | copy-start | bytes 1376260
  16.3 138.2 %all-gather.12.cloned.1.call-start = ((), (), s32[]{:S(2)}) async-start(), calls=%async_computation.3 | async-start | bytes 3784704 | tf_op jit(solution)/shard_map/all_gather | solution.py:116
  103.0 5.1 copy-start.14
  103.0 5.2 copy-start.18
  103.0 5.3 copy-start.15
  103.0 22.6 %all-to-all-start = ((bf16[16,256,128]{2,1,0:T(8,128)(2,1)}), bf16[16,256,128]{2,1,0:T(8,128)(2,1)S(1)}, u32[]{:S(2)}, u32[]{:S(2)}) async-start(bf16[16,256,128]{2,1,0:T(8,128)(2,1)} %bitcast.38), calls=%async_computation | async-start | bytes 2097152 | tf_op jit(solution)/shard_map/all_to_all | solution.py:142
  125.6 20.5 %all-to-all-start.1 = ((bf16[16,128,256]{2,1,0:T(8,128)(2,1)}), bf16[16,128,256]{2,1,0:T(8,128)(2,1)S(1)}, u32[]{:S(2)}, u32[]{:S(2)}) async-start(bf16[16,128,256]{2,1,0:T(8,128)(2,1)} %bitcast.41), calls=%async_computation.1 | async-start | bytes 2097152 | tf_op jit(solution)/shard_map/all_to_all | solution.py:141
  385.3 45.8 %all-gather.14.cloned.1.call-start = ((), (), s32[]{:S(2)}) async-start(), calls=%async_computation.5 | async-start | bytes 1114112 | tf_op jit(solution)/shard_map/while/body/eval_jaxpr/all_gather | solution.py:22
  386.0 99.5 %all-gather.16.cloned.1.call-start = ((), (), s32[]{:S(2)}) async-start(), calls=%async_computation.6 | async-start | bytes 2228224 | tf_op jit(solution)/shard_map/while/body/eval_jaxpr/all_gather | solution.py:22
  438.2 47.4 %copy-start.8 = (bf16[256,128]{1,0:T(8,128)(2,1)S(1)}, bf16[256,128]{1,0:T(8,128)(2,1)}, u32[]{:S(2)}) copy-start(bf16[256,128]{1,0:T(8,128)(2,1)} %bitcast_select_fusion.6) | copy-start | bytes 196612 | tf_op jit(solution)/shard_map/while
  441.1 48.3 %copy-start.2 = (bf16[256,2048]{1,0:T(8,128)(2,1)S(1)}, bf16[256,2048]{1,0:T(8,128)(2,1)}, u32[]{:S(2)}) copy-start(bf16[256,2048]{1,0:T(8,128)(2,1)} %all-gather.14.cloned.1.call-done) | copy-start | bytes 3145732 | tf_op jit(solution)/shard_map/while
  488.2 3.3 collective-permute-start
  491.5 45.7 %all-gather.14.cloned.1.call-start = ((), (), s32[]{:S(2)}) async-start(), calls=%async_computation.5 | async-start | bytes 1114112 | tf_op jit(solution)/shard_map/while/body/eval_jaxpr/all_gather | solution.py:22
  492.1 99.6 %all-gather.16.cloned.1.call-start = ((), (), s32[]{:S(2)}) async-start(), calls=%async_computation.6 | async-start | bytes 2228224 | tf_op jit(solution)/shard_map/while/body/eval_jaxpr/all_gather | solution.py:22
  544.3 47.4 %copy-start.8 = (bf16[256,128]{1,0:T(8,128)(2,1)S(1)}, bf16[256,128]{1,0:T(8,128)(2,1)}, u32[]{:S(2)}) copy-start(bf16[256,128]{1,0:T(8,128)(2,1)} %bitcast_select_fusion.6) | copy-start | bytes 196612 | tf_op jit(solution)/shard_map/while
  547.2 48.3 %copy-start.2 = (bf16[256,2048]{1,0:T(8,128)(2,1)S(1)}, bf16[256,2048]{1,0:T(8,128)(2,1)}, u32[]{:S(2)}) copy-start(bf16[256,2048]{1,0:T(8,128)(2,1)} %all-gather.14.cloned.1.call-done) | copy-start | bytes 3145732 | tf_op jit(solution)/shard_map/while
  594.2 3.3 collective-permute-start
  597.5 46.0 %all-gather.14.cloned.1.call-start = ((), (), s32[]{:S(2)}) async-start(), calls=%async_computation.5 | async-start | bytes 1114112 | tf_op jit(solution)/shard_map/while/body/eval_jaxpr/all_gather | solution.py:22
  598.3 99.8 %all-gather.16.cloned.1.call-start = ((), (), s32[]{:S(2)}) async-start(), calls=%async_computation.6 | async-start | bytes 2228224 | tf_op jit(solution)/shard_map/while/body/eval_jaxpr/all_gather | solution.py:22
  650.7 47.4 %copy-start.8 = (bf16[256,128]{1,0:T(8,128)(2,1)S(1)}, bf16[256,128]{1,0:T(8,128)(2,1)}, u32[]{:S(2)}) copy-start(bf16[256,128]{1,0:T(8,128)(2,1)} %bitcast_select_fusion.6) | copy-start | bytes 196612 | tf_op jit(solution)/shard_map/while
  653.6 48.3 %copy-start.2 = (bf16[256,2048]{1,0:T(8,128)(2,1)S(1)}, bf16[256,2048]{1,0:T(8,128)(2,1)}, u32[]{:S(2)}) copy-start(bf16[256,2048]{1,0:T(8,128)(2,1)} %all-gather.14.cloned.1.call-done) | copy-start | bytes 3145732 | tf_op jit(solution)/shard_map/while
  700.6 3.3 collective-permute-start
  703.9 4.8 copy-start.11
  704.0 4.8 copy-start.20
  708.8 46.0 %all-gather.18.cloned.1.call-start = ((), (), s32[]{:S(2)}) async-start(), calls=%async_computation.7 | async-start | bytes 1114112 | tf_op jit(solution)/shard_map/while/body/eval_jaxpr/all_gather | solution.py:22
  709.5 98.6 %all-gather.20.cloned.1.call-start = ((), (), s32[]{:S(2)}) async-start(), calls=%async_computation.8 | async-start | bytes 2228224 | tf_op jit(solution)/shard_map/while/body/eval_jaxpr/all_gather | solution.py:27
  765.5 4.8 copy-start.3
  780.2 27.9 %copy-start.7 = (bf16[256,128]{1,0:T(8,128)(2,1)S(1)}, bf16[256,128]{1,0:T(8,128)(2,1)}, u32[]{:S(2)}) copy-start(bf16[256,128]{1,0:T(8,128)(2,1)} %bitcast_select_fusion.7) | copy-start | bytes 196612 | tf_op jit(solution)/shard_map/while
  808.1 4.0 copy-start.4
  810.8 3.8 collective-permute-start.1
  815.9 46.8 %all-gather.18.cloned.1.call-start = ((), (), s32[]{:S(2)}) async-start(), calls=%async_computation.7 | async-start | bytes 1114112 | tf_op jit(solution)/shard_map/while/body/eval_jaxpr/all_gather | solution.py:22
  816.7 99.4 %all-gather.20.cloned.1.call-start = ((), (), s32[]{:S(2)}) async-start(), calls=%async_computation.8 | async-start | bytes 2228224 | tf_op jit(solution)/shard_map/while/body/eval_jaxpr/all_gather | solution.py:27
  873.5 4.8 copy-start.3
  888.1 27.9 %copy-start.7 = (bf16[256,128]{1,0:T(8,128)(2,1)S(1)}, bf16[256,128]{1,0:T(8,128)(2,1)}, u32[]{:S(2)}) copy-start(bf16[256,128]{1,0:T(8,128)(2,1)} %bitcast_select_fusion.7) | copy-start | bytes 196612 | tf_op jit(solution)/shard_map/while
  916.1 4.0 copy-start.4
  918.8 3.8 collective-permute-start.1
  923.9 46.8 %all-gather.18.cloned.1.call-start = ((), (), s32[]{:S(2)}) async-start(), calls=%async_computation.7 | async-start | bytes 1114112 | tf_op jit(solution)/shard_map/while/body/eval_jaxpr/all_gather | solution.py:22
  924.6 99.4 %all-gather.20.cloned.1.call-start = ((), (), s32[]{:S(2)}) async-start(), calls=%async_computation.8 | async-start | bytes 2228224 | tf_op jit(solution)/shard_map/while/body/eval_jaxpr/all_gather | solution.py:27
  981.5 4.8 copy-start.3
  996.1 27.9 %copy-start.7 = (bf16[256,128]{1,0:T(8,128)(2,1)S(1)}, bf16[256,128]{1,0:T(8,128)(2,1)}, u32[]{:S(2)}) copy-start(bf16[256,128]{1,0:T(8,128)(2,1)} %bitcast_select_fusion.7) | copy-start | bytes 196612 | tf_op jit(solution)/shard_map/while
  1024.0 4.0 copy-start.4
  1026.8 3.8 collective-permute-start.1
  1031.9 59.5 %all-reduce.3.cloned.1.call-start = ((), (), s32[]{:S(2)}) async-start(), calls=%async_computation.4 | async-start | bytes 1835008 | tf_op jit(solution)/shard_map/psum | solution.py:233
  1031.9 7.4 copy-start.6
  1039.3 55.7 %copy-start.1 = (bf16[1,896,256]{2,1,0:T(8,128)(2,1)S(1)}, bf16[1,896,256]{2,1,0:T(8,128)(2,1)}, u32[]{:S(2)}) copy-start(bf16[1,896,256]{2,1,0:T(8,128)(2,1)} %param.35) | copy-start | bytes 1376260
  (11 other events, 20.1 us)
Sparse Core Ops, SparseCore 0:
  16.4 79.8 all-gather.9
  103.2 51.2 all-gather.11
  388.8 42.2 all-gather.13
  439.2 46.3 all-gather.15
  494.6 42.4 all-gather.13
  545.2 46.3 all-gather.15
  601.0 42.5 all-gather.13
  651.6 46.3 all-gather.15
  712.3 42.5 all-gather.17
  761.7 46.3 all-gather.19
  819.4 43.2 all-gather.17
  869.6 46.3 all-gather.19
  927.4 43.3 all-gather.17
  977.6 46.3 all-gather.19
  1046.2 45.1 all-reduce.2
where the time goes:
time: 1110 us; the launch traced here: 1100 us
  waiting for transfers between devices  558 us (50%)
  local copies, waits for them, and re-layouts  296 us (27%)
  matrix products  120 us (11%)
  blocking collectives  68.5 us (6%)
  other arithmetic  26 us (2%)
  starting transfers between devices  17 us (2%)
  between operations  13.9 us (1%)
    all_gather x10, waiting for transfers between devices, collect(): return lax.all_gather(tensor, 'mp', axis=1, tiled=True)  468 us
    dynamic_update_slice x32, local copies, waits for them, and re-layouts, one_shard(): lax.dynamic_update_slice(whole_pool, shard_block, (row_start, col_start))  149 us
    all_gather x3, blocking collectives, collect_pair(): lax.all_gather(second, 'mp', axis=1, tiled=True)  68.5 us
    psum x1, waiting for transfers between devices, on_device(): lax.psum(key_sum.astype(jnp.bfloat16), 'dp').astype(jnp.float32)  45.3 us
    dynamic_slice x64, local copies, waits for them, and re-layouts, one_shard(): lax.dynamic_slice_in_dim(portion, position * shard_rows, shard_rows, 0)  34.4 us
    gather x1, local copies, waits for them, and re-layouts, on_device(): neighbours = jnp.take(whole_pool, global_rows, axis=0)  22.4 us
  transfers between devices with their start and end apart: 23, of which 17 were waited for; matrix products, arithmetic and copies ran while one was open for 10% of the time, Pallas kernels for 0%

commit v1 on v0

--- a/solution.py
+++ b/solution.py
@@ -8,6 +8,28 @@
 EPSILON = 1e-05
 
 
+def in_order(blocks, dim):
+    blocks = jnp.moveaxis(blocks, 0, dim)
+    shape = blocks.shape
+    return blocks.reshape(*shape[:dim], shape[dim] * shape[dim + 1], *shape[dim + 2 :])
+
+
+def gather_around(value, axis, dim):
+    size = lax.axis_size(axis)
+    pairs = [(i, (i + 1) % size) for i in range(size)]
+    back = [(b, a) for a, b in pairs]
+    lower, upper = ([], [])
+    for hop in range(size - 1):
+        if hop % 2 == 0:
+            lower.append(lax.ppermute(lower[-1] if lower else value, axis, pairs))
+        else:
+            upper.append(lax.ppermute(upper[-1] if upper else value, axis, back))
+    blocks = jnp.stack([*lower[::-1], value, *upper])
+    shift = lax.axis_index(axis) - len(lower)
+    blocks = blocks[(jnp.arange(size) - shift) % size]
+    return in_order(blocks, dim)
+
+
 def passed_along(value, axis, by):
     peers = lax.axis_size(axis)
     pairs = [(i, i + by) for i in range(peers) if 0 <= i + by < peers]
@@ -19,7 +41,7 @@
 
 
 def collect(tensor):
-    return lax.all_gather(tensor, "mp", axis=1, tiled=True)
+    return gather_around(tensor, "mp", 1)
 
 
 def collect_pair(first, second):

time: 1110 us -> 1440 us (1.30)
  starting transfers between devices: 17 us -> 402 us
  waiting for transfers between devices: 558 us -> 361 us
  local copies, waits for them, and re-layouts: 296 us -> 429 us
    all_gather x10 -> x0, waiting for transfers between devices: 468 us -> none  [collect(): return lax.all_gather(tensor, 'mp', axis=1, tiled=True)]
    ppermute x0 -> x150, starting transfers between devices: none -> 386 us  [the longest x70 380 us: gather_around(): upper.append(lax.ppermute(upper[-1] if upper else value, axis, back))]
    ppermute x0 -> x150, waiting for transfers between devices: none -> 272 us  [the longest x80 248 us: gather_around(): lower.append(lax.ppermute(lower[-1] if lower else value, axis, pairs))]
    while x51 -> x204, local copies, waits for them, and re-layouts: 8.08 us -> 50.6 us
    transpose x0 -> x10, local copies, waits for them, and re-layouts: none -> 25.3 us  [in_order(): blocks = jnp.moveaxis(blocks, 0, dim)]
    gather x0 -> x10, local copies, waits for them, and re-layouts: none -> 19.5 us  [gather_around(): blocks = blocks[(jnp.arange(size) - shift) % size]]
    unnamed x32 -> x73, local copies, waits for them, and re-layouts: 3.71 us -> 21.4 us
  transfers between devices with their start and end apart: 23 -> 163, of which waited for: 17 -> 82; matrix products, arithmetic and copies ran while one was open for 10% -> 13% of each run, Pallas kernels for 0% -> 0%
where the time goes in v1:
time: 1440 us; the launch traced here: 1430 us
  local copies, waits for them, and re-layouts  429 us (30%)
  starting transfers between devices  402 us (28%)
  waiting for transfers between devices  361 us (25%)
  matrix products  117 us (8%)
  blocking collectives  70.2 us (5%)
  other arithmetic  31.8 us (2%)
    ppermute x70, starting transfers between devices, gather_around(): upper.append(lax.ppermute(upper[-1] if upper else value, axis, back))  380 us
    ppermute x80, waiting for transfers between devices, gather_around(): lower.append(lax.ppermute(lower[-1] if lower else value, axis, pairs))  248 us
    dynamic_update_slice x32, local copies, waits for them, and re-layouts, one_shard(): lax.dynamic_update_slice(whole_pool, shard_block, (row_start, col_start))  149 us
    all_gather x3, blocking collectives, collect_pair(): lax.all_gather(second, 'mp', axis=1, tiled=True)  70.2 us
    while x204, local copies, waits for them, and re-layouts  50.6 us
    psum x1, waiting for transfers between devices, on_device(): lax.psum(key_sum.astype(jnp.bfloat16), 'dp').astype(jnp.float32)  45.4 us
    dynamic_slice x64, local copies, waits for them, and re-layouts, one_shard(): lax.dynamic_slice_in_dim(portion, position * shard_rows, shard_rows, 0)  34.4 us
  transfers between devices with their start and end apart: 163, of which 82 were waited for; matrix products, arithmetic and copies ran while one was open for 13% of the time, Pallas kernels for 0%

profile of v1, /device:TPU:0, one launch (start us, length us, event | category | flops | bytes accessed | tf_op | source)
XLA Modules:
  0.0 1428.6 jit_solution(11080687093535621749)
XLA Ops:
  17.2 16.8 %collective-permute-done.47 = bf16[1024,256]{1,0:T(8,128)(2,1)S(1)} collective-permute-done((bf16[1024,256]{1,0:T(8,128)(2,1)S(1)}, bf16[1024,256]{1,0:T(8,128)(2,1)S(1)}, u32[]{:S(2)}, u32[]{:S(2)}) %collective-permute-start.47) | collective-permute-done | bytes 524320 | tf_op jit(solution)/shard_map/ppermute | solution.py:24
  39.3 11.1 collective-permute-done.48
  55.7 10.2 collective-permute-done.49
  71.3 9.3 collective-permute-done.50
  86.1 8.4 collective-permute-done.51
  100.6 6.8 collective-permute-done.52
  107.5 5.9 collective-permute-start.60
  113.5 6.6 collective-permute-done.53
  120.7 5.8 collective-permute-start.61
  126.5 6.4 collective-permute-done.54
  150.7 8.2 gather_fusion.3
  158.9 12.3 copy.94
  171.2 5.6 fusion.103
  181.1 14.1 all-to-all-done
  202.7 9.8 all-to-all-done.1
  214.5 8.1 all-gather.6.cloned.1.call-done
  224.6 184.7 %while.55 = (s32[]{:T(128)}, bf16[2048,896]{1,0:T(8,128)(2,1)}, bf16[32768,56]{0,1:T(8,128)(2,1)}, s32[]{:T(128)}, s32[]{:T(128)}, /*index=5*/s32[]{:T(128)}, s3...) while((s32[]{:T(128)}, bf16[2048,896]{1,0:T(8,128)(2,1)}, ...), condition=%wide.region_2.3_spmd, body=%wide.region_1.2_spmd.sunk | while | flops 26 | bytes 688522 | solution.py:147
  409.4 22.5 %gather_fusion.4 = bf16[4096,896]{1,0:T(8,128)(2,1)} fusion(bf16[2048,896]{1,0:T(8,128)(2,1)} %get-tuple-element.883, s32[4096]{0:T(1024)S(1)} %broadcast_clamp_fusion), kind=kCustom, calls=%fused_computation.4 | custom fusion | bytes 14696448 | tf_op jit(solution)/shard_map/jit(_take)/gather | solution.py:148
  431.8 5.7 convolution_convert_fusion.4
  441.9 5.7 convolution_convert_fusion.5
  453.5 516.1 %while.56 = (s32[]{:T(128)}, bf16[256,128]{1,0:T(8,128)(2,1)S(1)}, bf16[2,256,2048]{2,1,0:T(8,128)(2,1)}, pred[]{:T(512)}, s32[]{:T(128)}, /*index=5*/bf16[2,256...) while((s32[]{:T(128)}, bf16[256,128]{1,0:T(8,128)(2,1)S(1)}, ...), condition=%wide.region_8.9_spmd, body=%wide.region_3.8_spmd.sunk | while | flops 677447680 | bytes 70481320 | solution.py:197
  456.3 6.1 collective-permute-done
  529.4 8.3 collective-permute-done.15
  562.8 5.6 collective-permute-start.26
  626.7 7.6 collective-permute-done
  701.2 8.3 collective-permute-done.15
  734.6 5.6 collective-permute-start.26
  798.5 7.6 collective-permute-done
  873.0 8.3 collective-permute-done.15
  906.4 5.6 collective-permute-start.26
  974.5 387.0 %while.57 = (s32[]{:T(128)}, bf16[256,128]{1,0:T(8,128)(2,1)S(1)}, bf16[2,4,512,2,128]{4,3,2,1,0:T(2,128)(2,1)}, bf16[2,4,512,2,128]{4,3,2,1,0:T(2,128)(2,1)}, p...) while((s32[]{:T(128)}, bf16[256,128]{1,0:T(8,128)(2,1)S(1)}, ...), condition=%wide.region_17.18_spmd, body=%wide.region_9.17_spmd.sunk | while | flops 1152263168 | bytes 91553216 | solution.py:238
  974.7 7.6 collective-permute-done.31
  1007.3 5.7 collective-permute-start.42
  1023.5 5.8 collective-permute-start.44
  1031.2 5.7 collective-permute-start.45
  1067.8 23.4 %all-gather.2 = bf16[16,1,256]{2,1,0:T(2,128)(2,1)S(1)} all-gather(bf16[1,1,256]{2,1,0:T(2,128)(2,1)S(1)} %reshape.700), channel_id=1, replica_groups=mesh['section'=2,'dp'=4,'mp'=16] {'mp'}, dimensions={0}, use_global_device_ids=true | all-gather | bytes 8704 | tf_op jit(solution)/shard_map/while/body/eval_jaxpr/all_gather | solution.py:50
  1104.4 7.0 collective-permute-done.31
  1136.4 5.7 collective-permute-start.42
  1152.2 5.7 collective-permute-start.44
  1160.2 5.8 collective-permute-start.45
  1196.9 23.4 %all-gather.2 = bf16[16,1,256]{2,1,0:T(2,128)(2,1)S(1)} all-gather(bf16[1,1,256]{2,1,0:T(2,128)(2,1)S(1)} %reshape.700), channel_id=1, replica_groups=mesh['section'=2,'dp'=4,'mp'=16] {'mp'}, dimensions={0}, use_global_device_ids=true | all-gather | bytes 8704 | tf_op jit(solution)/shard_map/while/body/eval_jaxpr/all_gather | solution.py:50
  1233.5 7.0 collective-permute-done.31
  1265.5 5.7 collective-permute-start.42
  1281.3 5.7 collective-permute-start.44
  1289.3 5.8 collective-permute-start.45
  1326.0 23.4 %all-gather.2 = bf16[16,1,256]{2,1,0:T(2,128)(2,1)S(1)} all-gather(bf16[1,1,256]{2,1,0:T(2,128)(2,1)S(1)} %reshape.700), channel_id=1, replica_groups=mesh['section'=2,'dp'=4,'mp'=16] {'mp'}, dimensions={0}, use_global_device_ids=true | all-gather | bytes 8704 | tf_op jit(solution)/shard_map/while/body/eval_jaxpr/all_gather | solution.py:50
  1361.6 7.4 fusion.97
  1372.8 45.4 %all-reduce.3.cloned.1.call-done = (bf16[1,896,256]{2,1,0:T(8,128)(2,1)}, bf16[1,896,256]{2,1,0:T(8,128)(2,1)}) async-done(((bf16[1,896,256]{2,1,0:T(8,128)(2,1)}, bf16[1,896,256]{2,1,0:T(8,128)(2,1)}), (bf16[1,896,256]{2,1,0:T(8,128)(2,1)}, bf16[1,896,256]{2,1,0:T(8,128)(2,1)})) %all-reduce.3.cloned.1.call-update) | async-done | bytes 917520 | tf_op jit(solution)/shard_map/psum | solution.py:255
  (883 shorter events, 972.4 us)
Async XLA Ops:
  7.2 215.4 %all-gather.6.cloned.1.call-start = ((), (), s32[]{:S(2)}) async-start(), calls=%async_computation.2 | async-start | bytes 3784704 | tf_op jit(solution)/shard_map/all_gather | solution.py:138
  15.4 18.6 %collective-permute-start.47 = (bf16[1024,256]{1,0:T(8,128)(2,1)S(1)}, bf16[1024,256]{1,0:T(8,128)(2,1)S(1)}, u32[]{:S(2)}, u32[]{:S(2)}) collective-permute-start(bf16[1024,256]{1,0:T(8,128)(2,1)S(1)} %fusion.111), channel_id=1, source_target_pairs={{0,1},{1,2},{2,3},{3,4},{4,5},{5,6},{6,7},{7,8},{8,9},{9,10},{10,1... | collective-permute-start | bytes 1572872 | tf_op jit(solution)/shard_map/ppermute | solution.py:24
  34.0 16.4 %collective-permute-start.48 = (bf16[1024,256]{1,0:T(8,128)(2,1)S(1)}, bf16[1024,256]{1,0:T(8,128)(2,1)S(1)}, u32[]{:S(2)}, u32[]{:S(2)}) collective-permute-start(bf16[1024,256]{1,0:T(8,128)(2,1)S(1)} %collective-permute-done.47), channel_id=1, source_target_pairs={{0,1},{1,2},{2,3},{3,4},{4,5},{5,6},{6,7},{7,8},{8,9},{9,10},{10,1... | collective-permute-start | bytes 1572872 | tf_op jit(solution)/shard_map/ppermute | solution.py:24
  34.0 16.4 %collective-permute-start.55 = (bf16[1024,256]{1,0:T(8,128)(2,1)S(1)}, bf16[1024,256]{1,0:T(8,128)(2,1)S(1)}, u32[]{:S(2)}, u32[]{:S(2)}) collective-permute-start(bf16[1024,256]{1,0:T(8,128)(2,1)S(1)} %fusion.111), channel_id=1, source_target_pairs={{1,0},{2,1},{3,2},{4,3},{5,4},{6,5},{7,6},{8,7},{9,8},{10,9},{11,1... | collective-permute-start | bytes 1572872 | tf_op jit(solution)/shard_map/ppermute | solution.py:26
  50.4 15.6 %collective-permute-start.49 = (bf16[1024,256]{1,0:T(8,128)(2,1)S(1)}, bf16[1024,256]{1,0:T(8,128)(2,1)S(1)}, u32[]{:S(2)}, u32[]{:S(2)}) collective-permute-start(bf16[1024,256]{1,0:T(8,128)(2,1)S(1)} %collective-permute-done.48), channel_id=1, source_target_pairs={{0,1},{1,2},{2,3},{3,4},{4,5},{5,6},{6,7},{7,8},{8,9},{9,10},{10,1... | collective-permute-start | bytes 1572872 | tf_op jit(solution)/shard_map/ppermute | solution.py:24
  50.4 15.6 %collective-permute-start.56 = (bf16[1024,256]{1,0:T(8,128)(2,1)S(1)}, bf16[1024,256]{1,0:T(8,128)(2,1)S(1)}, u32[]{:S(2)}, u32[]{:S(2)}) collective-permute-start(bf16[1024,256]{1,0:T(8,128)(2,1)S(1)} %collective-permute-done.55), channel_id=1, source_target_pairs={{1,0},{2,1},{3,2},{4,3},{5,4},{6,5},{7,6},{8,7},{9,8},{10,9},{11,1... | collective-permute-start | bytes 1572872 | tf_op jit(solution)/shard_map/ppermute | solution.py:26
  66.0 14.7 %collective-permute-start.50 = (bf16[1024,256]{1,0:T(8,128)(2,1)S(1)}, bf16[1024,256]{1,0:T(8,128)(2,1)S(1)}, u32[]{:S(2)}, u32[]{:S(2)}) collective-permute-start(bf16[1024,256]{1,0:T(8,128)(2,1)S(1)} %collective-permute-done.49), channel_id=1, source_target_pairs={{0,1},{1,2},{2,3},{3,4},{4,5},{5,6},{6,7},{7,8},{8,9},{9,10},{10,1... | collective-permute-start | bytes 1572872 | tf_op jit(solution)/shard_map/ppermute | solution.py:24
  66.0 14.7 %collective-permute-start.57 = (bf16[1024,256]{1,0:T(8,128)(2,1)S(1)}, bf16[1024,256]{1,0:T(8,128)(2,1)S(1)}, u32[]{:S(2)}, u32[]{:S(2)}) collective-permute-start(bf16[1024,256]{1,0:T(8,128)(2,1)S(1)} %collective-permute-done.56), channel_id=1, source_target_pairs={{1,0},{2,1},{3,2},{4,3},{5,4},{6,5},{7,6},{8,7},{9,8},{10,9},{11,1... | collective-permute-start | bytes 1572872 | tf_op jit(solution)/shard_map/ppermute | solution.py:26
  80.7 13.8 collective-permute-start.51
  80.7 13.8 collective-permute-start.58
  94.5 13.0 collective-permute-start.52
  95.3 12.2 collective-permute-start.59
  107.5 12.6 collective-permute-start.53
  107.5 13.1 collective-permute-start.60
  120.1 12.8 collective-permute-start.54
  120.7 29.1 %collective-permute-start.61 = (bf16[1024,256]{1,0:T(8,128)(2,1)}, bf16[1024,256]{1,0:T(8,128)(2,1)S(1)}, u32[]{:S(2)}, u32[]{:S(2)}) collective-permute-start(bf16[1024,256]{1,0:T(8,128)(2,1)} %collective-permute-done.60), channel_id=1, source_target_pairs={{1,0},{2,1},{3,2},{4,3},{5,4},{6,5},{7,6},{8,7},{9,8},{10,9},{11,1... | collective-permute-start | bytes 1572872 | tf_op jit(solution)/shard_map/ppermute | solution.py:26
  176.9 18.3 %all-to-all-start = ((bf16[16,256,128]{2,1,0:T(8,128)(2,1)}), bf16[16,256,128]{2,1,0:T(8,128)(2,1)S(1)}, u32[]{:S(2)}, u32[]{:S(2)}) async-start(bf16[16,256,128]{2,1,0:T(8,128)(2,1)} %bitcast.111), calls=%async_computation | async-start | bytes 2097152 | tf_op jit(solution)/shard_map/all_to_all | solution.py:164
  195.2 17.3 %all-to-all-start.1 = ((bf16[16,128,256]{2,1,0:T(8,128)(2,1)}), bf16[16,128,256]{2,1,0:T(8,128)(2,1)S(1)}, u32[]{:S(2)}, u32[]{:S(2)}) async-start(bf16[16,128,256]{2,1,0:T(8,128)(2,1)} %bitcast.114), calls=%async_computation.1 | async-start | bytes 2097152 | tf_op jit(solution)/shard_map/all_to_all | solution.py:163
  562.8 9.3 collective-permute-start.19
  562.8 9.3 collective-permute-start.26
  572.1 14.4 %collective-permute-start.27 = (bf16[256,256]{1,0:T(8,128)(2,1)S(1)}, bf16[256,256]{1,0:T(8,128)(2,1)}, u32[]{:S(2)}, u32[]{:S(2)}) collective-permute-start(bf16[256,256]{1,0:T(8,128)(2,1)S(1)} %collective-permute-done.26), channel_id=1, source_target_pairs={{1,0},{2,1},{3,2},{4,3},{5,4},{6,5},{7,6},{8,7},{9,8},{10,9},{11,1... | collective-permute-start | bytes 393224 | tf_op jit(solution)/shard_map/while/body/eval_jaxpr/ppermute | solution.py:26
  580.5 11.4 collective-permute-start.21
  586.5 8.9 collective-permute-start.28
  591.9 8.9 collective-permute-start.22
  595.5 19.8 %collective-permute-start.29 = (bf16[256,256]{1,0:T(8,128)(2,1)}, bf16[256,256]{1,0:T(8,128)(2,1)S(1)}, u32[]{:S(2)}, u32[]{:S(2)}) collective-permute-start(bf16[256,256]{1,0:T(8,128)(2,1)} %collective-permute-done.28), channel_id=1, source_target_pairs={{1,0},{2,1},{3,2},{4,3},{5,4},{6,5},{7,6},{8,7},{9,8},{10,9},{11,1... | collective-permute-start | bytes 393224 | tf_op jit(solution)/shard_map/while/body/eval_jaxpr/ppermute | solution.py:26
  734.6 9.4 collective-permute-start.19
  734.6 9.4 collective-permute-start.26
  744.0 14.4 %collective-permute-start.27 = (bf16[256,256]{1,0:T(8,128)(2,1)S(1)}, bf16[256,256]{1,0:T(8,128)(2,1)}, u32[]{:S(2)}, u32[]{:S(2)}) collective-permute-start(bf16[256,256]{1,0:T(8,128)(2,1)S(1)} %collective-permute-done.26), channel_id=1, source_target_pairs={{1,0},{2,1},{3,2},{4,3},{5,4},{6,5},{7,6},{8,7},{9,8},{10,9},{11,1... | collective-permute-start | bytes 393224 | tf_op jit(solution)/shard_map/while/body/eval_jaxpr/ppermute | solution.py:26
  752.4 11.4 collective-permute-start.21
  758.4 8.9 collective-permute-start.28
  763.7 8.9 collective-permute-start.22
  767.3 19.8 %collective-permute-start.29 = (bf16[256,256]{1,0:T(8,128)(2,1)}, bf16[256,256]{1,0:T(8,128)(2,1)S(1)}, u32[]{:S(2)}, u32[]{:S(2)}) collective-permute-start(bf16[256,256]{1,0:T(8,128)(2,1)} %collective-permute-done.28), channel_id=1, source_target_pairs={{1,0},{2,1},{3,2},{4,3},{5,4},{6,5},{7,6},{8,7},{9,8},{10,9},{11,1... | collective-permute-start | bytes 393224 | tf_op jit(solution)/shard_map/while/body/eval_jaxpr/ppermute | solution.py:26
  897.9 8.6 collective-permute-start.18
  897.9 8.6 collective-permute-start.25
  906.4 9.4 collective-permute-start.19
  906.4 9.4 collective-permute-start.26
  915.9 14.4 %collective-permute-start.27 = (bf16[256,256]{1,0:T(8,128)(2,1)S(1)}, bf16[256,256]{1,0:T(8,128)(2,1)}, u32[]{:S(2)}, u32[]{:S(2)}) collective-permute-start(bf16[256,256]{1,0:T(8,128)(2,1)S(1)} %collective-permute-done.26), channel_id=1, source_target_pairs={{1,0},{2,1},{3,2},{4,3},{5,4},{6,5},{7,6},{8,7},{9,8},{10,9},{11,1... | collective-permute-start | bytes 393224 | tf_op jit(solution)/shard_map/while/body/eval_jaxpr/ppermute | solution.py:26
  924.2 11.4 collective-permute-start.21
  930.3 8.9 collective-permute-start.28
  935.6 8.9 collective-permute-start.22
  939.2 19.8 %collective-permute-start.29 = (bf16[256,256]{1,0:T(8,128)(2,1)}, bf16[256,256]{1,0:T(8,128)(2,1)S(1)}, u32[]{:S(2)}, u32[]{:S(2)}) collective-permute-start(bf16[256,256]{1,0:T(8,128)(2,1)} %collective-permute-done.28), channel_id=1, source_target_pairs={{1,0},{2,1},{3,2},{4,3},{5,4},{6,5},{7,6},{8,7},{9,8},{10,9},{11,1... | collective-permute-start | bytes 393224 | tf_op jit(solution)/shard_map/while/body/eval_jaxpr/ppermute | solution.py:26
  974.5 120.7 %all-gather.8.cloned.1.call-start = ((), (), s32[]{:S(2)}) async-start(), calls=%async_computation.4 | async-start | bytes 2228224 | tf_op jit(solution)/shard_map/while/body/eval_jaxpr/all_gather | solution.py:49
  989.9 10.1 collective-permute-start.40
  1103.1 121.3 %all-gather.8.cloned.1.call-start = ((), (), s32[]{:S(2)}) async-start(), calls=%async_computation.4 | async-start | bytes 2228224 | tf_op jit(solution)/shard_map/while/body/eval_jaxpr/all_gather | solution.py:49
  1118.9 10.1 collective-permute-start.40
  1232.2 121.3 %all-gather.8.cloned.1.call-start = ((), (), s32[]{:S(2)}) async-start(), calls=%async_computation.4 | async-start | bytes 2228224 | tf_op jit(solution)/shard_map/while/body/eval_jaxpr/all_gather | solution.py:49
  1248.0 10.1 collective-permute-start.40
  1361.5 56.7 %all-reduce.3.cloned.1.call-start = ((), (), s32[]{:S(2)}) async-start(), calls=%async_computation.3 | async-start | bytes 1835008 | tf_op jit(solution)/shard_map/psum | solution.py:255
  (173 other events, 2354.9 us)
Sparse Core Ops, SparseCore 0:
  177.0 45.4 all-gather.5
  1046.7 48.5 all-gather.7
  1175.8 48.5 all-gather.7
  1304.9 48.5 all-gather.7
  1372.9 45.1 all-reduce.2
